TPU v7x, 32 devices: a whole 2x2x4 slice. The times are simulated.
32 devices in a mesh: gx: 4 (over z), gy: 2 (over y), gz: 4 (over x, core).
Axes of the slice: x: 2, y: 2, z: 4, core: 2. Of those that a mesh axis runs over, the one named last changes fastest.
Arguments:
- adjoint_guess: float32 [2, 20, 128, 1024], P(None, 'gz', 'gy', 'gx'), may hold values from -6 to 6
- viscosity: float32 [20, 128, 1024], P('gz', 'gy', 'gx'), may hold values from 0.2 to 2
- friction: float32 [128, 1024], P('gy', 'gx'), may hold values from 0.2 to 5
- base_velocity: float32 [2, 128, 1024], P(None, 'gy', 'gx'), may hold values from -6 to 6
- surface_slope: float32 [2, 128, 1024], P(None, 'gy', 'gx'), may hold values from -6 to 6
- ice_mask: int32 [128, 1024], P('gy', 'gx'), may hold values 0 or 1
- pixel_misfit: float32 [524288], P(('gx', 'gy', 'gz')), may hold values from -6 to 6
- pixel_look: float32 [524288], P(('gx', 'gy', 'gz')), may hold values from -3.140625 to 3.140625
- pixel_tile: int32 [524288, 1], P(('gx', 'gy', 'gz')), may hold values from 0 to 7; in each aligned block of 16384 rows (0 to 16383, 16384 to 32767, ...) at most 4096 rows name the same one
- pixel_cell: int32 [524288], P(('gx', 'gy', 'gz')), may hold values from 0 to 16383
- pixel_count: int32 [32], P(('gx', 'gy', 'gz')), may hold values from 1 to 16384, 393216 in all
Outputs:
- adjoint: float32 [2, 20, 128, 1024], P(None, 'gz', 'gy', 'gx')
- sensitivity_maps: float32 [2, 128, 1024], P(None, ('gy', 'gz'), 'gx')
Inputs may be any that keep to these rules, and one draw needn't show every extreme that they name: `pixel_tile`: among the rows of one device no tile is named more than 4096 times, a bound that some block reaches. `pixel_count`: rows of a device from its count on are padding.
All inputs are finite; a program needn't handle non-finite values. No bound on the sum of `ice_mask` on one device may be relied on, other than what follows from the above.
Results may differ from a plain program's by a relative error of at most 0.00002.
Values sent between devices are 32-bit elements; how exact they have to be, the bound alone decides.
A program may use at most 128 MiB of HBM per device.

v0:
```python
import jax
import jax.numpy as jnp
from jax import lax
from jax.sharding import PartitionSpec as P

ITERS = 2
OMEGA = 0.6
VERTICAL = 4.0


def padded_2(block, sides, width):
    for axis, dim in sides:
        count = lax.axis_size(axis)
        forward = [(i, i + 1) for i in range(count - 1)]
        backward = [(target, source) for source, target in forward]
        low = lax.ppermute(
            lax.slice_in_dim(block, block.shape[dim] - width, None, axis=dim), axis, forward
        )
        high = lax.ppermute(lax.slice_in_dim(block, 0, width, axis=dim), axis, backward)
        block = jnp.concatenate([low, block, high], axis=dim)
    return block


def box_apply(padded, visc_pad, mask_east, mask_north, mask_upper):
    first = padded[0]
    second = padded[1]
    base_a = first[:-1, :-1, :-1]
    base_b = second[:-1, :-1, :-1]
    east_a = (first[:-1, :-1, 1:] - base_a) * mask_east
    east_b = (second[:-1, :-1, 1:] - base_b) * mask_east
    north_a = (first[:-1, 1:, :-1] - base_a) * mask_north
    north_b = (second[:-1, 1:, :-1] - base_b) * mask_north
    upper_a = (first[1:, :-1, :-1] - base_a) * mask_upper
    upper_b = (second[1:, :-1, :-1] - base_b) * mask_upper
    visc_box = visc_pad[:-1, :-1, :-1]
    along_x = visc_box * (4.0 * east_a + 2.0 * north_b) * mask_east
    along_y = visc_box * (4.0 * north_b + 2.0 * east_a) * mask_north
    shear = visc_box * (north_a + east_b)
    shear_x = shear * mask_east
    shear_y = shear * mask_north
    vert_a = VERTICAL * visc_box * upper_a
    vert_b = VERTICAL * visc_box * upper_b
    result_a = (
        along_x[1:, 1:, :-1]
        - along_x[1:, 1:, 1:]
        + (shear_y[1:, :-1, 1:] - shear_y[1:, 1:, 1:])
        + (vert_a[:-1, 1:, 1:] - vert_a[1:, 1:, 1:])
    )
    result_b = (
        along_y[1:, :-1, 1:]
        - along_y[1:, 1:, 1:]
        + (shear_x[1:, 1:, :-1] - shear_x[1:, 1:, 1:])
        + (vert_b[:-1, 1:, 1:] - vert_b[1:, 1:, 1:])
    )
    return jnp.stack([result_a, result_b])


def body(
    adjoint_guess,
    viscosity,
    friction,
    base_velocity,
    surface_slope,
    ice_mask,
    pixel_misfit,
    pixel_look,
    pixel_tile,
    pixel_cell,
    pixel_count,
):
    layer_local = adjoint_guess.shape[1]
    rows_local = adjoint_guess.shape[2]
    cols_local = adjoint_guess.shape[3]
    count_x = lax.axis_size("gx")
    count_y = lax.axis_size("gy")
    count_z = lax.axis_size("gz")
    layer_total = layer_local * count_z
    full_x = cols_local * count_x
    full_y = rows_local * count_y
    tile_total = count_x * count_y
    per_device = pixel_misfit.shape[0]
    capacity = 2 * per_device // tile_total
    mask_float = ice_mask.astype(jnp.float32)
    live = jnp.arange(per_device, dtype=jnp.int32) < pixel_count[0]
    values = jnp.where(live, pixel_misfit, jnp.float32(0.0))
    dest_tile = pixel_tile[:, 0]
    one_hot = (dest_tile[:, None] == jnp.arange(tile_total, dtype=jnp.int32)[None, :]).astype(
        jnp.int32
    )
    running = jnp.cumsum(one_hot, axis=0)
    slot_index = jnp.sum(one_hot * running, axis=1) - 1
    position = dest_tile * capacity + slot_index
    payload = jnp.stack(
        [values * jnp.cos(pixel_look), values * jnp.sin(pixel_look), pixel_cell.astype(jnp.float32)]
    )
    outbox = jnp.zeros((3, tile_total * capacity), jnp.float32).at[:, position].set(payload)
    inbox = lax.all_to_all(
        outbox.reshape(3, tile_total, capacity),
        ("gx", "gy"),
        split_axis=1,
        concat_axis=1,
        tiled=True,
    )
    received = inbox.reshape(3, tile_total * capacity)
    cell_ids = received[2].astype(jnp.int32)
    forcing = jnp.zeros((2, rows_local * cols_local), jnp.float32).at[:, cell_ids].add(received[:2])
    forcing = forcing.reshape(2, rows_local, cols_local)
    forcing = lax.psum(forcing, "gz") * mask_float[None]
    layer_ids = lax.axis_index("gz") * layer_local + jnp.arange(layer_local, dtype=jnp.int32)
    bottom = (layer_ids == 0).astype(jnp.float32)[:, None, None]
    top = (layer_ids == layer_total - 1).astype(jnp.float32)[:, None, None]
    rhs = forcing[:, None, :, :] * top[None]
    basal = friction[None] * bottom
    damping = OMEGA / (18.0 * viscosity + basal)
    east_ids = lax.axis_index("gx") * cols_local + jnp.arange(cols_local + 1, dtype=jnp.int32) - 1
    north_ids = lax.axis_index("gy") * rows_local + jnp.arange(rows_local + 1, dtype=jnp.int32) - 1
    upper_ids = (
        lax.axis_index("gz") * layer_local + jnp.arange(layer_local + 1, dtype=jnp.int32) - 1
    )
    mask_east = (east_ids + 1 < full_x).astype(jnp.float32)[None, None, :]
    mask_north = (north_ids + 1 < full_y).astype(jnp.float32)[None, :, None]
    mask_upper = (upper_ids + 1 < layer_total).astype(jnp.float32)[:, None, None]
    adjoint = adjoint_guess
    for sweep in range(ITERS):
        stacked = jnp.concatenate([adjoint, viscosity[None]], axis=0)
        rims = padded_2(stacked, (("gx", 3), ("gy", 2), ("gz", 1)), 1)
        image = (
            box_apply(rims[:2], rims[2], mask_east, mask_north, mask_upper) + basal[None] * adjoint
        )
        adjoint = adjoint + damping[None] * (rhs - image)
    on_base = (lax.axis_index("gz") == 0).astype(jnp.float32)
    fric_term = (
        -on_base
        * mask_float
        * friction
        * (base_velocity[0] * adjoint[0, 0] + base_velocity[1] * adjoint[1, 0])
    )
    drive_term = (
        0.25
        * mask_float
        * jnp.sum(surface_slope[0][None] * adjoint[0] + surface_slope[1][None] * adjoint[1], axis=0)
    )
    maps = lax.psum_scatter(
        jnp.stack([fric_term, drive_term]), "gz", scatter_dimension=1, tiled=True
    )
    return (adjoint, maps)


def solution(mesh):
    return jax.shard_map(
        body,
        mesh=mesh,
        in_specs=(
            P(None, "gz", "gy", "gx"),
            P("gz", "gy", "gx"),
            P("gy", "gx"),
            P(None, "gy", "gx"),
            P(None, "gy", "gx"),
            P("gy", "gx"),
            P(("gx", "gy", "gz")),
            P(("gx", "gy", "gz")),
            P(("gx", "gy", "gz"), None),
            P(("gx", "gy", "gz")),
            P(("gx", "gy", "gz")),
        ),
        out_specs=(P(None, "gz", "gy", "gx"), P(None, ("gy", "gz"), "gx")),
        check_vma=False,
    )
```

profile of v0, /device:TPU:0, one launch (start us, length us, event | category | flops | bytes accessed | tf_op | source)
XLA Modules:
  0.0 580.0 jit_solution(1309384241617030706)
XLA Ops:
  7.2 2.4 fusion.57
  9.5 5.0 collective-permute-start
  18.6 5.1 copy.28
  25.2 47.4 %scatter_custom_fusion = f32[3,32768]{0,1:T(8,128)} fusion(s32[16384]{0:T(1024)S(1)} %bitcast.116, f32[16384,3]{1,0:T(8,128)} %copy.28, f32[]{:T(128)} %constant.26.clone.1), kind=kCustom, calls=%fused_computation.2 | custom fusion | bytes 393728 | tf_op jit(solution)/shard_map/scatter | solution.py:96
  72.6 9.9 %copy.29 = f32[3,8,4096]{2,0,1:T(4,128)} copy(f32[3,8,4096]{0,2,1:T(8,128)} %bitcast.96) | data formatting | bytes 786432 | tf_op jit(solution)/shard_map/reshape | solution.py:98
  82.5 7.0 %all-to-all-start = ((f32[3,8,4096]{2,0,1:T(4,128)}), f32[3,8,4096]{2,0,1:T(4,128)S(1)}, u32[]{:S(2)}, u32[]{:S(2)}) async-start(f32[3,8,4096]{2,0,1:T(4,128)} %copy.29), calls=%async_computation | async-start | bytes 1048576 | tf_op jit(solution)/shard_map/all_to_all | solution.py:97
  90.3 3.9 collective-permute-start.2
  95.7 4.2 collective-permute-done.3
  103.6 3.6 collective-permute-done.5
  108.0 1.8 broadcast_multiply_fusion.2
  112.1 8.3 %copy.30 = f32[32768,2]{1,0:T(8,128)} copy(f32[32768,2]{0,1:T(2,128)S(1)} %bitcast.107) | data formatting | bytes 524288 | tf_op jit(solution)/shard_map/slice | solution.py:106
  120.7 188.6 %scatter_custom_fusion.1 = f32[2,16384]{0,1:T(8,128)} fusion(s32[32768]{0:T(1024)S(1)} %bitcast.115, f32[32768,2]{1,0:T(8,128)} %copy.30, f32[]{:T(128)} %constant.26.clone.1), kind=kCustom, calls=%fused_computation.5 | custom fusion | flops 65536 | bytes 131584 | tf_op jit(solution)/shard_map/scatter-add | solution.py:106
  309.4 3.4 fusion.69
  312.8 182.0 %all-reduce.2.cloned.1.call-done = f32[2,64,256]{0,2,1:T(8,128)} async-done(((f32[2,64,256]{0,2,1:T(8,128)}), f32[2,64,256]{0,2,1:T(8,128)}) %all-reduce.2.cloned.1.call-update) | async-done | bytes 131088 | tf_op jit(solution)/shard_map/psum | solution.py:108
  494.8 7.9 %broadcast_multiply_fusion = f32[2,64,256]{0,2,1:T(8,128)} fusion(f32[2,64,256]{0,2,1:T(8,128)} %all-reduce.2.cloned.1.call-done, f32[64,256]{1,0:T(8,128)S(1)} %convert_element_type.67), kind=kLoop, calls=%fused_computation.4 | loop fusion | flops 32768 | bytes 327680 | tf_op jit(solution)/shard_map/mul | solution.py:108
  502.7 5.2 copy.31
  508.4 3.4 collective-permute-start.6
  513.1 8.8 %collective-permute-done.6 = f32[3,5,64,1]{3,2,1,0:T(8,128)S(1)} collective-permute-done((f32[3,5,64,1]{3,2,1,0:T(8,128)S(1)}, f32[3,5,64,1]{3,2,1,0:T(8,128)S(1)}, u32[]{:S(2)}, u32[]{:S(2)}) %collective-permute-start.6) | collective-permute-done | bytes 3872 | tf_op jit(solution)/shard_map/ppermute | solution.py:16
  521.9 4.1 collective-permute-done.7
  527.3 4.0 collective-permute-start.8
  532.6 4.7 collective-permute-done.9
  540.0 1.5 collective-permute-start.11
  541.6 3.2 collective-permute-done.11
  550.1 23.0 %reduce-scatter.2.cloned.1.call-done = f32[2,16,256]{2,1,0:T(8,128)} async-done(((f32[2,64,256]{2,1,0:T(8,128)}), f32[2,16,256]{2,1,0:T(8,128)}) %reduce-scatter.2.cloned.1.call-update) | async-done | bytes 32784 | tf_op jit(solution)/shard_map/reduce_scatter | solution.py:143
  (91 shorter events, 26.4 us)
Async XLA Ops:
  9.5 80.1 %collective-permute-start = (f32[3,5,64,1]{3,2,1,0:T(8,128)}, f32[3,5,64,1]{3,2,1,0:T(8,128)S(1)}, u32[]{:S(2)}, u32[]{:S(2)}) collective-permute-start(f32[3,5,64,1]{3,2,1,0:T(8,128)} %get-tuple-element.26), channel_id=1, source_target_pairs={{0,8},{8,16},{16,24},{1,9},{9,17},{17,25},{2,10},{10,18},{18,26},{... | collective-permute-start | bytes 11528 | tf_op jit(solution)/shard_map/ppermute | solution.py:16
  14.5 75.2 %collective-permute-start.1 = (f32[3,5,64,1]{3,2,1,0:T(8,128)}, f32[3,5,64,1]{3,2,1,0:T(8,128)S(1)}, u32[]{:S(2)}, u32[]{:S(2)}) collective-permute-start(f32[3,5,64,1]{3,2,1,0:T(8,128)} %get-tuple-element.27), channel_id=1, source_target_pairs={{8,0},{16,8},{24,16},{9,1},{17,9},{25,17},{10,2},{18,10},{26,18},{... | collective-permute-start | bytes 11528 | tf_op jit(solution)/shard_map/ppermute | solution.py:19
  18.6 5.1 copy-start.7
  72.6 17.1 %copy-start = (f32[5,64,256]{2,1,0:T(8,128)S(1)}, f32[5,64,256]{2,1,0:T(8,128)}, u32[]{:S(2)}) copy-start(f32[5,64,256]{2,1,0:T(8,128)} %param.12) | copy-start | bytes 983044
  72.6 17.1 %copy-start.1 = (f32[2,5,64,256]{3,2,1,0:T(8,128)S(1)}, f32[2,5,64,256]{3,2,1,0:T(8,128)}, u32[]{:S(2)}) copy-start(f32[2,5,64,256]{3,2,1,0:T(8,128)} %param.11) | copy-start | bytes 1966084
  82.5 13.0 %copy-start.8 = (s32[64,256]{1,0:T(8,128)S(1)}, s32[64,256]{1,0:T(8,128)}, u32[]{:S(2)}) copy-start(s32[64,256]{1,0:T(8,128)} %param.16) | copy-start | bytes 196612
  82.5 29.5 %all-to-all-start = ((f32[3,8,4096]{2,0,1:T(4,128)}), f32[3,8,4096]{2,0,1:T(4,128)S(1)}, u32[]{:S(2)}, u32[]{:S(2)}) async-start(f32[3,8,4096]{2,0,1:T(4,128)} %copy.29), calls=%async_computation | async-start | bytes 1048576 | tf_op jit(solution)/shard_map/all_to_all | solution.py:97
  89.5 405.3 %all-reduce.2.cloned.1.call-start = ((), (), s32[]{:S(2)}) async-start(), calls=%async_computation.2 | async-start | bytes 16777216 | tf_op jit(solution)/shard_map/psum | solution.py:108
  90.3 5.4 collective-permute-start.2
  94.2 5.7 collective-permute-start.3
  95.5 7.9 %copy-start.9 = (f32[64,256]{1,0:T(8,128)S(1)}, f32[64,256]{1,0:T(8,128)}, u32[]{:S(2)}) copy-start(f32[64,256]{1,0:T(8,128)} %param.13) | copy-start | bytes 196612
  100.6 3.0 collective-permute-start.4
  101.9 5.2 collective-permute-start.5
  103.5 404.4 %copy-start.3 = (f32[5,64,256]{2,1,0:T(8,128)}, f32[5,64,256]{2,1,0:T(8,128)S(1)}, u32[]{:S(2)}) copy-start(f32[5,64,256]{2,1,0:T(8,128)S(1)} %get-tuple-element.36) | copy-start | bytes 983044
  103.6 404.4 %copy-start.5 = (f32[5,64,256]{2,1,0:T(8,128)}, f32[5,64,256]{2,1,0:T(8,128)S(1)}, u32[]{:S(2)}) copy-start(f32[5,64,256]{2,1,0:T(8,128)S(1)} %get-tuple-element.37) | copy-start | bytes 983044
  309.3 263.8 %reduce-scatter.2.cloned.1.call-start = ((), (), s32[]{:S(2)}) async-start(), calls=%async_computation.3 | async-start | bytes 163840 | tf_op jit(solution)/shard_map/reduce_scatter | solution.py:143
  508.4 13.5 %collective-permute-start.6 = (f32[3,5,64,1]{3,2,1,0:T(8,128)S(1)}, f32[3,5,64,1]{3,2,1,0:T(8,128)S(1)}, u32[]{:S(2)}, u32[]{:S(2)}) collective-permute-start(f32[3,5,64,1]{3,2,1,0:T(8,128)S(1)} %get-tuple-element.24), channel_id=1, source_target_pairs={{0,8},{8,16},{16,24},{1,9},{9,17},{17,25},{2,10},{10,18},{18,26},{... | collective-permute-start | bytes 11528 | tf_op jit(solution)/shard_map/ppermute | solution.py:16
  511.8 14.3 %collective-permute-start.7 = (f32[3,5,64,1]{3,2,1,0:T(8,128)S(1)}, f32[3,5,64,1]{3,2,1,0:T(8,128)S(1)}, u32[]{:S(2)}, u32[]{:S(2)}) collective-permute-start(f32[3,5,64,1]{3,2,1,0:T(8,128)S(1)} %get-tuple-element.25), channel_id=1, source_target_pairs={{8,0},{16,8},{24,16},{9,1},{17,9},{25,17},{10,2},{18,10},{26,18},{... | collective-permute-start | bytes 11528 | tf_op jit(solution)/shard_map/ppermute | solution.py:19
  527.3 5.3 collective-permute-start.8
  531.2 6.0 %collective-permute-start.9 = (f32[3,5,1,258]{3,2,1,0:T(1,128)}, f32[3,5,1,258]{3,2,1,0:T(1,128)}, u32[]{:S(2)}, u32[]{:S(2)}) collective-permute-start(f32[3,5,1,258]{3,2,1,0:T(1,128)} %get-tuple-element.21), channel_id=1, source_target_pairs={{4,0},{5,1},{6,2},{7,3},{12,8},{13,9},{14,10},{15,11},{20,16},{21,... | collective-permute-start | bytes 46448 | tf_op jit(solution)/shard_map/ppermute | solution.py:19
  532.5 9.0 %copy-start.10 = (f32[2,64,256]{2,1,0:T(8,128)S(1)}, f32[2,64,256]{2,1,0:T(8,128)}, u32[]{:S(2)}) copy-start(f32[2,64,256]{2,1,0:T(8,128)} %param.15) | copy-start | bytes 393220
  538.7 2.9 collective-permute-start.10
  540.0 4.7 collective-permute-start.11
  548.8 24.3 %copy-start.2 = (f32[2,5,64,256]{3,2,1,0:T(8,128)}, f32[2,5,64,256]{3,2,1,0:T(8,128)S(1)}, u32[]{:S(2)}) copy-start(f32[2,5,64,256]{3,2,1,0:T(8,128)S(1)} %fusion.51) | copy-start | bytes 1966084
  (3 other events, 3.0 us)
Sparse Core Ops, SparseCore 0:
  309.4 185.3 all-reduce.1
  550.2 22.8 reduce-scatter.1
where the time goes:
time: 581 us; the launch traced here: 580 us
  waiting for transfers between devices  234 us (40%)
  other arithmetic  219 us (38%)
  local copies, waits for them, and re-layouts  78 us (13%)
  starting transfers between devices  34.1 us (6%)
  between operations  15.2 us (3%)
    scatter-add x1, other arithmetic, body(): jnp.zeros((2, rows_local * cols_local), jnp.float32).at[:, cell_ids]  189 us
    psum x1, waiting for transfers between devices, body(): forcing = lax.psum(forcing, 'gz') * mask_float[None]  182 us
    scatter x1, local copies, waits for them, and re-layouts, body(): jnp.zeros((3, tile_total * capacity), jnp.float32).at[:, position]  47.4 us
    reduce_scatter x1, waiting for transfers between devices, body(): lax.psum_scatter(jnp.stack([fric_term, drive_term]), 'gz', scatter_dimens...  23 us
    ppermute x6, waiting for transfers between devices, padded_2(): lax.ppermute(lax.slice_in_dim(block, 0, width, axis=dim), axis, backward)  19.8 us
    ppermute x6, starting transfers between devices, padded_2(): lax.ppermute(lax.slice_in_dim(block, block.shape[dim] - width, None, axis...  18.9 us
  transfers between devices with their start and end apart: 15, of which 9 were waited for; matrix products, arithmetic and copies ran while one was open for 13% of the time, Pallas kernels for 0%

commit v1 on v0

--- a/solution.py
+++ b/solution.py
@@ -1,3 +1,4 @@
+import functools
 import jax
 import jax.numpy as jnp
 from jax import lax
@@ -6,6 +7,14 @@
 ITERS = 2
 OMEGA = 0.6
 VERTICAL = 4.0
+
+
+def keep_up_spots(shard_in, a_name):
+    local_next = lax.all_gather(shard_in, a_name)
+    return jnp.sum(local_next, 0)
+
+
+grid_supply = functools.partial(keep_up_spots, a_name="gz")
 
 
 def padded_2(block, sides, width):
@@ -105,7 +114,7 @@
     cell_ids = received[2].astype(jnp.int32)
     forcing = jnp.zeros((2, rows_local * cols_local), jnp.float32).at[:, cell_ids].add(received[:2])
     forcing = forcing.reshape(2, rows_local, cols_local)
-    forcing = lax.psum(forcing, "gz") * mask_float[None]
+    forcing = grid_supply(forcing) * mask_float[None]
     layer_ids = lax.axis_index("gz") * layer_local + jnp.arange(layer_local, dtype=jnp.int32)
     bottom = (layer_ids == 0).astype(jnp.float32)[:, None, None]
     top = (layer_ids == layer_total - 1).astype(jnp.float32)[:, None, None]

time: 581 us -> 442 us (0.76)
  waiting for transfers between devices: 234 us -> 53.7 us
  starting transfers between devices: 34.1 us -> 59 us
  local copies, waits for them, and re-layouts: 78 us -> 89 us
  blocking collectives: 0 us -> 10.7 us
  other arithmetic: 219 us -> 213 us
    psum x1 -> x0, waiting for transfers between devices: 182 us -> none  [body(): forcing = lax.psum(forcing, 'gz') * mask_float[None]]
    ppermute x6, starting transfers between devices: 18.9 us -> 43.8 us  [padded_2(): lax.ppermute(lax.slice_in_dim(block, block.shape[dim] - width, None, axis...]
    all_gather x0 -> x1, blocking collectives: none -> 10.7 us  [keep_up_spots(): local_next = lax.all_gather(shard_in, a_name)]
  transfers between devices with their start and end apart: 15 -> 14, of which waited for: 9 -> 9; matrix products, arithmetic and copies ran while one was open for 13% -> 16% of each run, Pallas kernels for 0% -> 0%
where the time goes in v1:
time: 442 us; the launch traced here: 441 us
  other arithmetic  213 us (48%)
  local copies, waits for them, and re-layouts  89 us (20%)
  starting transfers between devices  59 us (13%)
  waiting for transfers between devices  53.7 us (12%)
  between operations  15.3 us (3%)
  blocking collectives  10.7 us (2%)
    scatter-add x1, other arithmetic, body(): jnp.zeros((2, rows_local * cols_local), jnp.float32).at[:, cell_ids]  189 us
    scatter x1, local copies, waits for them, and re-layouts, body(): jnp.zeros((3, tile_total * capacity), jnp.float32).at[:, position]  47.4 us
    ppermute x6, starting transfers between devices, padded_2(): lax.ppermute(lax.slice_in_dim(block, block.shape[dim] - width, None, axis...  43.8 us
    reduce_scatter x1, waiting for transfers between devices, body(): lax.psum_scatter(jnp.stack([fric_term, drive_term]), 'gz', scatter_dimens...  24.1 us
    ppermute x6, waiting for transfers between devices, padded_2(): lax.ppermute(lax.slice_in_dim(block, 0, width, axis=dim), axis, backward)  19.4 us
    all_gather x1, blocking collectives, keep_up_spots(): local_next = lax.all_gather(shard_in, a_name)  10.7 us
    ppermute x6, waiting for transfers between devices, padded_2(): lax.ppermute(lax.slice_in_dim(block, block.shape[dim] - width, None, axis...  10.2 us
    reshape x1, local copies, waits for them, and re-layouts, body(): outbox.reshape(3, tile_total, capacity)  9.94 us
  transfers between devices with their start and end apart: 14, of which 9 were waited for; matrix products, arithmetic and copies ran while one was open for 16% of the time, Pallas kernels for 0%

profile of v1, /device:TPU:0, one launch (start us, length us, event | category | flops | bytes accessed | tf_op | source)
XLA Modules:
  0.0 440.9 jit_solution(14025563960086484744)
XLA Ops:
  8.5 5.0 %collective-permute-start = (f32[3,5,64,1]{3,2,1,0:T(8,128)S(1)}, f32[3,5,64,1]{3,2,1,0:T(8,128)S(1)}, u32[]{:S(2)}, u32[]{:S(2)}) collective-permute-start(f32[3,5,64,1]{3,2,1,0:T(8,128)S(1)} %get-tuple-element.26), channel_id=1, source_target_pairs={{0,8},{8,16},{16,24},{1,9},{9,17},{17,25},{2,10},{10,18},{18,26},{... | collective-permute-start | bytes 11528 | tf_op jit(solution)/shard_map/ppermute | solution.py:25
  17.6 5.1 %copy.28 = f32[16384,3]{1,0:T(8,128)} copy(f32[16384,3]{0,1:T(4,128)S(1)} %maximum_bitcast_fusion) | data formatting | bytes 393216 | tf_op jit(solution)/shard_map/stack | solution.py:102
  24.2 47.4 %scatter_custom_fusion = f32[3,32768]{0,1:T(8,128)} fusion(s32[16384]{0:T(1024)S(1)} %bitcast.116, f32[16384,3]{1,0:T(8,128)} %copy.28, f32[]{:T(128)} %constant.26.clone.1), kind=kCustom, calls=%fused_computation.2 | custom fusion | bytes 393728 | tf_op jit(solution)/shard_map/scatter | solution.py:105
  71.6 9.9 %copy.29 = f32[3,8,4096]{2,0,1:T(4,128)} copy(f32[3,8,4096]{0,2,1:T(8,128)} %bitcast.96) | data formatting | bytes 786432 | tf_op jit(solution)/shard_map/reshape | solution.py:107
  81.5 7.0 %all-to-all-start = ((f32[3,8,4096]{2,0,1:T(4,128)}), f32[3,8,4096]{2,0,1:T(4,128)}, u32[]{:S(2)}, u32[]{:S(2)}) async-start(f32[3,8,4096]{2,0,1:T(4,128)} %copy.29), calls=%async_computation | async-start | bytes 1048576 | tf_op jit(solution)/shard_map/all_to_all | solution.py:106
  89.8 3.9 collective-permute-start.2
  95.2 4.2 collective-permute-done.3
  101.4 1.5 collective-permute-start.5
  103.1 3.6 collective-permute-done.5
  110.7 8.3 %copy.30 = f32[32768,2]{1,0:T(8,128)} copy(f32[32768,2]{0,1:T(2,128)S(1)} %bitcast.107) | data formatting | bytes 524288 | tf_op jit(solution)/shard_map/slice | solution.py:115
  120.3 188.6 %scatter_custom_fusion.1 = f32[2,16384]{0,1:T(8,128)} fusion(s32[32768]{0:T(1024)S(1)} %bitcast.115, f32[32768,2]{1,0:T(8,128)} %copy.30, f32[]{:T(128)} %constant.26.clone.1), kind=kCustom, calls=%fused_computation.5 | custom fusion | flops 65536 | bytes 131584 | tf_op jit(solution)/shard_map/scatter-add | solution.py:115
  308.9 5.2 %copy.31 = f32[1,2,64,256]{3,2,1,0:T(8,128)S(1)} copy(f32[1,2,64,256]{1,3,2,0:T(8,128)} %bitcast.97) | data formatting | bytes 262144 | tf_op jit(solution)/shard_map/all_gather;reshape | solution.py:13
  314.1 10.7 %all_gather.3 = f32[4,2,64,256]{3,2,1,0:T(8,128)S(1)} all-gather(f32[1,2,64,256]{3,2,1,0:T(8,128)S(1)} %copy.31), channel_id=1, replica_groups=mesh['gx'=4,'gy'=2,'gz'=4] {'gz'}, dimensions={0}, use_global_device_ids=true | all-gather | bytes 655360 | tf_op jit(solution)/shard_map/all_gather | solution.py:13
  324.8 4.7 %copy.34 = f32[2,64,256]{0,2,1:T(8,128)} copy(f32[2,64,256]{2,1,0:T(8,128)S(1)} %reduce_sum.28) | data formatting | bytes 262144
  329.5 8.0 %broadcast_multiply_fusion = f32[2,64,256]{0,2,1:T(8,128)} fusion(f32[2,64,256]{0,2,1:T(8,128)} %copy.34, f32[64,256]{1,0:T(8,128)S(1)} %convert_element_type.67), kind=kLoop, calls=%fused_computation.4 | loop fusion | flops 32768 | bytes 327680 | tf_op jit(solution)/shard_map/mul | solution.py:117
  337.5 5.2 %copy.33 = f32[2,64,256]{2,1,0:T(8,128)S(1)} copy(f32[2,64,256]{0,2,1:T(8,128)} %broadcast_multiply_fusion) | data formatting | bytes 262144 | tf_op jit(solution)/shard_map/mul | solution.py:117
  343.1 31.0 %collective-permute-start.6 = (f32[3,5,64,1]{3,2,1,0:T(8,128)S(1)}, f32[3,5,64,1]{3,2,1,0:T(8,128)S(1)}, u32[]{:S(2)}, u32[]{:S(2)}) collective-permute-start(f32[3,5,64,1]{3,2,1,0:T(8,128)S(1)} %get-tuple-element.24), channel_id=1, source_target_pairs={{0,8},{8,16},{16,24},{1,9},{9,17},{17,25},{2,10},{10,18},{18,26},{... | collective-permute-start | bytes 11528 | tf_op jit(solution)/shard_map/ppermute | solution.py:25
  375.5 9.6 %collective-permute-done.6 = f32[3,5,64,1]{3,2,1,0:T(8,128)S(1)} collective-permute-done((f32[3,5,64,1]{3,2,1,0:T(8,128)S(1)}, f32[3,5,64,1]{3,2,1,0:T(8,128)S(1)}, u32[]{:S(2)}, u32[]{:S(2)}) %collective-permute-start.6) | collective-permute-done | bytes 3872 | tf_op jit(solution)/shard_map/ppermute | solution.py:25
  385.1 4.1 collective-permute-done.7
  393.5 4.2 collective-permute-done.9
  399.8 1.5 collective-permute-start.11
  401.3 3.3 collective-permute-done.11
  404.6 1.4 fusion.15
  410.0 24.1 %reduce-scatter.2.cloned.1.call-done = f32[2,16,256]{2,1,0:T(8,128)} async-done(((f32[2,64,256]{2,1,0:T(8,128)}), f32[2,16,256]{2,1,0:T(8,128)}) %reduce-scatter.2.cloned.1.call-update) | async-done | bytes 32784 | tf_op jit(solution)/shard_map/reduce_scatter | solution.py:152
  (99 shorter events, 28.1 us)
Async XLA Ops:
  8.5 80.6 %collective-permute-start = (f32[3,5,64,1]{3,2,1,0:T(8,128)S(1)}, f32[3,5,64,1]{3,2,1,0:T(8,128)S(1)}, u32[]{:S(2)}, u32[]{:S(2)}) collective-permute-start(f32[3,5,64,1]{3,2,1,0:T(8,128)S(1)} %get-tuple-element.26), channel_id=1, source_target_pairs={{0,8},{8,16},{16,24},{1,9},{9,17},{17,25},{2,10},{10,18},{18,26},{... | collective-permute-start | bytes 11528 | tf_op jit(solution)/shard_map/ppermute | solution.py:25
  13.5 75.6 %collective-permute-start.1 = (f32[3,5,64,1]{3,2,1,0:T(8,128)S(1)}, f32[3,5,64,1]{3,2,1,0:T(8,128)S(1)}, u32[]{:S(2)}, u32[]{:S(2)}) collective-permute-start(f32[3,5,64,1]{3,2,1,0:T(8,128)S(1)} %get-tuple-element.27), channel_id=1, source_target_pairs={{8,0},{16,8},{24,16},{9,1},{17,9},{25,17},{10,2},{18,10},{26,18},{... | collective-permute-start | bytes 11528 | tf_op jit(solution)/shard_map/ppermute | solution.py:28
  17.6 5.1 %copy-start.7 = (s32[16384,1]{0,1:T(1,128)S(1)}, s32[16384,1]{0,1:T(1,128)}, u32[]{:S(2)}) copy-start(s32[16384,1]{0,1:T(1,128)} %param.19) | copy-start | bytes 196612
  71.6 17.6 %copy-start = (f32[5,64,256]{2,1,0:T(8,128)S(1)}, f32[5,64,256]{2,1,0:T(8,128)}, u32[]{:S(2)}) copy-start(f32[5,64,256]{2,1,0:T(8,128)} %param.12) | copy-start | bytes 983044
  71.6 17.6 %copy-start.1 = (f32[2,5,64,256]{3,2,1,0:T(8,128)S(1)}, f32[2,5,64,256]{3,2,1,0:T(8,128)}, u32[]{:S(2)}) copy-start(f32[2,5,64,256]{3,2,1,0:T(8,128)} %param.11) | copy-start | bytes 1966084
  81.5 13.5 %copy-start.8 = (s32[64,256]{1,0:T(8,128)S(1)}, s32[64,256]{1,0:T(8,128)}, u32[]{:S(2)}) copy-start(s32[64,256]{1,0:T(8,128)} %param.16) | copy-start | bytes 196612
  81.5 28.0 %all-to-all-start = ((f32[3,8,4096]{2,0,1:T(4,128)}), f32[3,8,4096]{2,0,1:T(4,128)}, u32[]{:S(2)}, u32[]{:S(2)}) async-start(f32[3,8,4096]{2,0,1:T(4,128)} %copy.29), calls=%async_computation | async-start | bytes 1048576 | tf_op jit(solution)/shard_map/all_to_all | solution.py:106
  88.6 345.5 %reduce-scatter.2.cloned.1.call-start = ((), (), s32[]{:S(2)}) async-start(), calls=%async_computation.2 | async-start | bytes 163840 | tf_op jit(solution)/shard_map/reduce_scatter | solution.py:152
  89.8 5.4 %collective-permute-start.2 = (f32[3,5,1,258]{3,2,1,0:T(1,128)S(1)}, f32[3,5,1,258]{3,2,1,0:T(1,128)S(1)}, u32[]{:S(2)}, u32[]{:S(2)}) collective-permute-start(f32[3,5,1,258]{3,2,1,0:T(1,128)S(1)} %get-tuple-element.22), channel_id=1, source_target_pairs={{0,4},{1,5},{2,6},{3,7},{8,12},{9,13},{10,14},{11,15},{16,20},{17,... | collective-permute-start | bytes 46448 | tf_op jit(solution)/shard_map/ppermute | solution.py:25
  93.7 5.7 %collective-permute-start.3 = (f32[3,5,1,258]{3,2,1,0:T(1,128)S(1)}, f32[3,5,1,258]{3,2,1,0:T(1,128)S(1)}, u32[]{:S(2)}, u32[]{:S(2)}) collective-permute-start(f32[3,5,1,258]{3,2,1,0:T(1,128)S(1)} %get-tuple-element.23), channel_id=1, source_target_pairs={{4,0},{5,1},{6,2},{7,3},{12,8},{13,9},{14,10},{15,11},{20,16},{21,... | collective-permute-start | bytes 46448 | tf_op jit(solution)/shard_map/ppermute | solution.py:28
  95.0 7.9 %copy-start.9 = (f32[64,256]{1,0:T(8,128)S(1)}, f32[64,256]{1,0:T(8,128)}, u32[]{:S(2)}) copy-start(f32[64,256]{1,0:T(8,128)} %param.13) | copy-start | bytes 196612
  95.0 7.9 %copy-start.15 = (f32[5]{0:T(128)S(1)}, f32[5]{0:T(128)}, u32[]{:S(2)}) copy-start(f32[5]{0:T(128)} %get-tuple-element.41) | copy-start | bytes 64
  100.1 3.0 collective-permute-start.4
  101.4 5.2 %collective-permute-start.5 = (f32[3,1,66,258]{3,2,1,0:T(8,128)S(1)}, f32[3,1,66,258]{3,2,1,0:T(8,128)S(1)}, u32[]{:S(2)}, u32[]{:S(2)}) collective-permute-start(f32[3,1,66,258]{3,2,1,0:T(8,128)S(1)} %get-tuple-element.19), channel_id=1, source_target_pairs={{1,0},{2,1},{3,2},{5,4},{6,5},{7,6},{9,8},{10,9},{11,10},{13,12},{... | collective-permute-start | bytes 613016 | tf_op jit(solution)/shard_map/ppermute | solution.py:28
  103.1 239.6 %copy-start.3 = (f32[5,64,256]{2,1,0:T(8,128)}, f32[5,64,256]{2,1,0:T(8,128)S(1)}, u32[]{:S(2)}) copy-start(f32[5,64,256]{2,1,0:T(8,128)S(1)} %get-tuple-element.36) | copy-start | bytes 983044
  103.1 239.6 %copy-start.5 = (f32[5,64,256]{2,1,0:T(8,128)}, f32[5,64,256]{2,1,0:T(8,128)S(1)}, u32[]{:S(2)}) copy-start(f32[5,64,256]{2,1,0:T(8,128)S(1)} %get-tuple-element.37) | copy-start | bytes 983044
  343.1 42.0 %collective-permute-start.6 = (f32[3,5,64,1]{3,2,1,0:T(8,128)S(1)}, f32[3,5,64,1]{3,2,1,0:T(8,128)S(1)}, u32[]{:S(2)}, u32[]{:S(2)}) collective-permute-start(f32[3,5,64,1]{3,2,1,0:T(8,128)S(1)} %get-tuple-element.24), channel_id=1, source_target_pairs={{0,8},{8,16},{16,24},{1,9},{9,17},{17,25},{2,10},{10,18},{18,26},{... | collective-permute-start | bytes 11528 | tf_op jit(solution)/shard_map/ppermute | solution.py:25
  374.2 15.1 %collective-permute-start.7 = (f32[3,5,64,1]{3,2,1,0:T(8,128)S(1)}, f32[3,5,64,1]{3,2,1,0:T(8,128)S(1)}, u32[]{:S(2)}, u32[]{:S(2)}) collective-permute-start(f32[3,5,64,1]{3,2,1,0:T(8,128)S(1)} %get-tuple-element.25), channel_id=1, source_target_pairs={{8,0},{16,8},{24,16},{9,1},{17,9},{25,17},{10,2},{18,10},{26,18},{... | collective-permute-start | bytes 11528 | tf_op jit(solution)/shard_map/ppermute | solution.py:28
  390.5 3.0 collective-permute-start.8
  391.8 5.9 %collective-permute-start.9 = (f32[3,5,1,258]{3,2,1,0:T(1,128)}, f32[3,5,1,258]{3,2,1,0:T(1,128)S(1)}, u32[]{:S(2)}, u32[]{:S(2)}) collective-permute-start(f32[3,5,1,258]{3,2,1,0:T(1,128)} %get-tuple-element.21), channel_id=1, source_target_pairs={{4,0},{5,1},{6,2},{7,3},{12,8},{13,9},{14,10},{15,11},{20,16},{21,... | collective-permute-start | bytes 46448 | tf_op jit(solution)/shard_map/ppermute | solution.py:28
  393.1 8.2 %copy-start.11 = (f32[2,64,256]{2,1,0:T(8,128)S(1)}, f32[2,64,256]{2,1,0:T(8,128)}, u32[]{:S(2)}) copy-start(f32[2,64,256]{2,1,0:T(8,128)} %param.15) | copy-start | bytes 393220
  398.4 2.9 collective-permute-start.10
  399.8 4.8 %collective-permute-start.11 = (f32[3,1,66,258]{3,2,1,0:T(8,128)S(1)}, f32[3,1,66,258]{3,2,1,0:T(8,128)S(1)}, u32[]{:S(2)}, u32[]{:S(2)}) collective-permute-start(f32[3,1,66,258]{3,2,1,0:T(8,128)S(1)} %get-tuple-element.17), channel_id=1, source_target_pairs={{1,0},{2,1},{3,2},{5,4},{6,5},{7,6},{9,8},{10,9},{11,10},{13,12},{... | collective-permute-start | bytes 613016 | tf_op jit(solution)/shard_map/ppermute | solution.py:28
  408.6 25.4 %copy-start.2 = (f32[2,5,64,256]{3,2,1,0:T(8,128)}, f32[2,5,64,256]{3,2,1,0:T(8,128)S(1)}, u32[]{:S(2)}) copy-start(f32[2,5,64,256]{3,2,1,0:T(8,128)S(1)} %fusion.51) | copy-start | bytes 1966084
  (6 other events, 9.6 us)
Sparse Core Ops, SparseCore 0:
  410.1 23.8 reduce-scatter.1
